TPU v7x, 32 devices: a whole 2x2x4 slice. The times are simulated.
32 devices in a mesh: shard: 8 (over z, y), tensor: 4 (over x, core).
Axes of the slice: x: 2, y: 2, z: 4, core: 2. Of those that a mesh axis runs over, the one named last changes fastest.
Arguments:
- grad_parts: float32 [4, 4, 768, 768], P('tensor', None, 'shard'), may hold values from -0.6 to 0.6
- adam_v: float32 [4, 768, 768], P(None, 'shard', 'tensor'), may hold values from 0.01 to 0.2
- left_stat: float32 [8, 768, 768], P('shard', 'tensor'), may hold values from -6 to 6
- right_stat: float32 [8, 768, 768], P('shard', 'tensor'), may hold values from -6 to 6
- left_root: bfloat16 [8, 768, 768], P('shard', 'tensor'), as said below
- right_root: bfloat16 [8, 768, 768], P('shard', 'tensor'), as said below
- owner: int32 [4], replicated, may hold values from 0 to 7, as said below
- vec_parts: float32 [4, 4, 768], P('tensor', None, 'shard'), may hold values from -0.6 to 0.6
- vec_m: float32 [4, 768], P(None, 'shard'), may hold values from -0.3 to 0.3
- vec_v: float32 [4, 768], P(None, 'shard'), may hold values from 0.01 to 0.2
Outputs:
- update: float32 [4, 768, 768], P(None, 'shard', 'tensor')
- new_adam_v: float32 [4, 768, 768], P(None, 'shard', 'tensor')
- new_left: float32 [8, 768, 768], P('shard', 'tensor')
- new_right: float32 [8, 768, 768], P('shard', 'tensor')
- new_vec_m: float32 [4, 768], P(None, 'shard')
- new_vec_v: float32 [4, 768], P(None, 'shard')
- vec_step: float32 [4, 768], P(None, 'shard')
Inputs may be any that keep to these rules, and one draw needn't show every extreme that they name: owner holds 4 distinct slot numbers: no slot owns two tiles. `left_root`: each slot's matrix is symmetric. `right_root`: each slot's matrix is symmetric.
All inputs are finite; a program needn't handle non-finite values.
Results may differ from a plain program's by a relative error of at most 0.0003.
Values may be sent and summed in bfloat16 or wider, within the bound.
No kernel may reach another device: no remote copies, remote signals or barrier semaphores. Data moves between devices by JAX's collectives and lax.ppermute only.
A program may use at most 64 MiB of HBM per device.

v0:
```python
import jax
import jax.numpy as jnp
from jax import lax
from jax.sharding import PartitionSpec as P

BETA_ONE = 0.9
BETA_TWO = 0.95
STAT_DECAY = 0.95
STEP_COUNT = 10.0
EPSILON = 1e-08
NORM_EPS = 1e-06
HIGH = lax.Precision.HIGHEST


def local(
    grad_parts, adam_v, left_stat, right_stat, left_root, right_root, owner, vec_parts, vec_m, vec_v
):
    shards = lax.axis_size("shard")
    tiles = owner.shape[0]
    grad = lax.psum_scatter(grad_parts[0], "tensor", scatter_dimension=2, tiled=True)
    rows_dev = grad.shape[1]
    cols_dev = grad.shape[2]
    new_adam_v = BETA_TWO * adam_v + (1.0 - BETA_TWO) * grad * grad
    bias_two = 1.0 - BETA_TWO**STEP_COUNT
    adam_dir = grad / (jnp.sqrt(new_adam_v / bias_two) + EPSILON)
    adam_sq = jnp.sum(adam_dir * adam_dir, axis=(1, 2))
    vec_grad = lax.psum(vec_parts[0], "tensor")
    new_vec_m = BETA_ONE * vec_m + (1.0 - BETA_ONE) * vec_grad
    new_vec_v = BETA_TWO * vec_v + (1.0 - BETA_TWO) * vec_grad * vec_grad
    bias_one = 1.0 - BETA_ONE**STEP_COUNT
    vec_step = new_vec_m / bias_one / (jnp.sqrt(new_vec_v / bias_two) + EPSILON)
    slot_hot = (jnp.arange(shards, dtype=jnp.int32)[:, None] == owner[None, :]).astype(jnp.float32)
    outgoing = jnp.dot(slot_hot, grad.reshape(tiles, rows_dev * cols_dev), precision=HIGH)
    outgoing = outgoing.reshape(shards, rows_dev, cols_dev)
    arrived = lax.all_to_all(outgoing, "shard", split_axis=0, concat_axis=1, tiled=True)[0]
    whole = lax.all_gather(arrived, "tensor", axis=1, tiled=True)
    start = lax.axis_index("tensor") * cols_dev
    tile_rows = lax.dynamic_slice_in_dim(whole, start, cols_dev, 0)
    new_left = STAT_DECAY * left_stat[0] + (1.0 - STAT_DECAY) * jnp.dot(
        tile_rows, whole.T, precision=HIGH
    )
    new_right = STAT_DECAY * right_stat[0] + (1.0 - STAT_DECAY) * jnp.dot(
        arrived.T, whole, precision=HIGH
    )
    right_full = lax.all_gather(right_root[0], "tensor", axis=0, tiled=True).astype(jnp.float32)
    left_part = jnp.dot(left_root[0].astype(jnp.float32), whole, precision=HIGH)
    row_block = jnp.dot(left_part, right_full, precision=HIGH)
    direction = lax.all_to_all(row_block[None], "tensor", split_axis=2, concat_axis=1, tiled=True)[
        0
    ]
    returned = lax.all_to_all(
        direction.reshape(shards, rows_dev, cols_dev),
        "shard",
        split_axis=0,
        concat_axis=0,
        tiled=True,
    )
    update = jnp.dot(slot_hot.T, returned.reshape(shards, rows_dev * cols_dev), precision=HIGH)
    update = update.reshape(tiles, rows_dev, cols_dev)
    shampoo_local = jnp.sum(update * update, axis=(1, 2))
    adam_total, shampoo_total = lax.psum((adam_sq, shampoo_local), ("shard", "tensor"))
    graft = jnp.sqrt(adam_total) / (jnp.sqrt(shampoo_total) + NORM_EPS)
    update = graft[:, None, None] * update
    return (update, new_adam_v, new_left[None], new_right[None], new_vec_m, new_vec_v, vec_step)


def solution(mesh):
    in_specs = (
        P("tensor", None, "shard", None),
        P(None, "shard", "tensor"),
        P("shard", "tensor", None),
        P("shard", "tensor", None),
        P("shard", "tensor", None),
        P("shard", "tensor", None),
        P(),
        P("tensor", None, "shard"),
        P(None, "shard"),
        P(None, "shard"),
    )
    out_specs = (
        P(None, "shard", "tensor"),
        P(None, "shard", "tensor"),
        P("shard", "tensor", None),
        P("shard", "tensor", None),
        P(None, "shard"),
        P(None, "shard"),
        P(None, "shard"),
    )
    return jax.shard_map(local, mesh=mesh, in_specs=in_specs, out_specs=out_specs, check_vma=False)
```

profile of v0, /device:TPU:0, one launch (start us, length us, event | category | flops | bytes accessed | tf_op | source)
XLA Modules:
  0.0 205.5 jit_solution(14201237901707531373)
XLA Ops:
  7.2 1.8 copy.38
  9.0 1.8 reshape.39
  10.9 28.5 %reduce-scatter.4.cloned.1.call-done = f32[192,384]{1,0:T(8,128)} async-done(((f32[768,384]{1,0:T(8,128)}), f32[192,384]{1,0:T(8,128)}) %reduce-scatter.4.cloned.1.call-update) | async-done | bytes 294928
  39.4 1.2 reshape.40
  41.4 0.8 fusion.9
  42.4 25.5 %all_to_all.29 = f32[8,96,192]{2,1,0:T(8,128)S(1)} all-to-all(f32[8,96,192]{2,1,0:T(8,128)S(1)} %copy.30), channel_id=1, replica_groups=mesh['shard'=8,'tensor'=4] {'shard'}, dimensions={0} | all-to-all | bytes 1179648 | tf_op jit(solution)/shard_map/all_to_all | solution.py:35
  67.9 1.1 copy.37
  69.7 21.6 %all-gather.4.cloned.1.call-done = f32[768,768]{0,1:T(8,128)} async-done(((f32[768,192]{0,1:T(8,128)}), f32[768,768]{0,1:T(8,128)}) %all-gather.4.cloned.1.call-update) | async-done | bytes 2359312 | tf_op jit(solution)/shard_map/all_gather | solution.py:36
  91.3 3.1 %fusion.11 = f32[768,192]{0,1:T(8,128)S(1)} fusion(f32[768,768]{0,1:T(8,128)} %all-gather.4.cloned.1.call-done, bf16[1,192,768]{2,1,0:T(8,128)(2,1)S(1)} %copy-done), kind=kOutput, calls=%fused_computation.17 | convolution fusion | flops 1358954496 | bytes 3244032 | tf_op jit(solution)/shard_map/dot_general | solution.py:46
  94.4 16.0 %all-gather.6.cloned.1.call-done = bf16[1,768,768]{2,1,0:T(8,128)(2,1)} async-done(((bf16[1,192,768]{2,1,0:T(8,128)(2,1)}), bf16[1,768,768]{2,1,0:T(8,128)(2,1)}) %all-gather.6.cloned.1.call-update) | async-done | bytes 1179664 | tf_op jit(solution)/shard_map/all_gather | solution.py:45
  110.4 2.1 %convolution_bitcast_fusion = f32[1,192,768]{2,1,0:T(8,128)S(1)} fusion(f32[768,192]{0,1:T(8,128)S(1)} %fusion.11, bf16[1,768,768]{2,1,0:T(8,128)(2,1)} %all-gather.6.cloned.1.call-done), kind=kOutput, calls=%fused_computation.6 | convolution fusion | flops 1358954496 | bytes 2359296 | tf_op jit(solution)/shard_map/dot_general | solution.py:47
  113.2 14.1 %all_to_all.30 = f32[1,192,768]{1,0,2:T(1,128)S(1)} all-to-all(f32[1,192,768]{1,0,2:T(1,128)S(1)} %copy.32), channel_id=1, replica_groups=mesh['shard'=8,'tensor'=4] {'tensor'}, dimensions={2} | all-to-all | bytes 1179648 | tf_op jit(solution)/shard_map/all_to_all | solution.py:48
  127.7 1.5 all_to_all.23
  129.2 2.3 %copy.34 = f32[1,4,192,192]{3,2,1,0:T(8,128)} copy(f32[1,4,192,192]{3,1,2,0:T(4,128)} %bitcast.44) | data formatting | bytes 1179648 | tf_op jit(solution)/shard_map/all_to_all | solution.py:48
  131.5 5.5 %all-to-all-start.2 = ((f32[8,96,192]{2,1,0:T(8,128)}), f32[8,96,192]{2,1,0:T(8,128)}, u32[]{:S(2)}, u32[]{:S(2)}) async-start(f32[8,96,192]{2,1,0:T(8,128)} %bitcast.43), calls=%async_computation.2 | async-start | bytes 1572864 | tf_op jit(solution)/shard_map/all_to_all | solution.py:51
  137.0 6.2 %psum.23 = f32[4,96]{1,0:T(4,128)S(1)} all-reduce(f32[4,96]{1,0:T(4,128)S(1)} %bitcast.49), channel_id=1, replica_groups=mesh['shard'=8,'tensor'=4] {'tensor'}, use_global_device_ids=true, to_apply=%region_5.0 | all-reduce | flops 384 | bytes 3072 | tf_op jit(solution)/shard_map/psum | solution.py:27
  143.9 2.1 %multiply_reduce_fusion.1 = (f32[4]{0:T(128)S(1)}, f32[4,96,192]{2,1,0:T(8,128)}) fusion(f32[4,96,192]{2,1,0:T(8,128)} %copy-done.2, f32[4,96,192]{2,1,0:T(8,128)} %param.11), kind=kLoop, calls=%fused_computation.16 | loop fusion | flops 663548 | bytes 884752 | tf_op jit(solution)/shard_map/reduce_sum | solution.py:26
  146.0 4.0 %fusion.3 = f32[1,192,768]{2,1,0:T(8,128)} fusion(f32[768,768]{0,1:T(8,128)S(1)} %copy-done.1, s32[]{:T(128)S(6)} %select_n.3, f32[1,192,768]{2,1,0:T(8,128)} %param.12), kind=kOutput, calls=%fused_computation.5 | convolution fusion | flops 1359396864 | bytes 4325380 | tf_op jit(solution)/shard_map/dot_general | solution.py:39
  150.0 4.8 %fusion.1 = f32[1,192,768]{2,1,0:T(8,128)} fusion(f32[768,192]{1,0:T(8,128)S(1)} %bitcast.41, f32[768,768]{0,1:T(8,128)S(1)} %copy-done.1, f32[1,192,768]{2,1,0:T(8,128)S(1)} %copy-done.3), kind=kOutput, calls=%fused_computation.2 | convolution fusion | flops 1359396864 | bytes 4128768 | tf_op jit(solution)/shard_map/dot_general | solution.py:42
  154.8 2.2 %all-to-all-done.2 = f32[8,96,192]{2,1,0:T(8,128)} async-done(((f32[8,96,192]{2,1,0:T(8,128)}), f32[8,96,192]{2,1,0:T(8,128)}, u32[]{:S(2)}, u32[]{:S(2)}) %all-to-all-start.2) | async-done | bytes 589856 | tf_op jit(solution)/shard_map/all_to_all | solution.py:51
  157.0 1.4 reshape.36
  158.8 1.1 multiply_reduce_fusion
  159.9 38.0 %all-reduce = (f32[4]{0:T(128)S(1)}, f32[4]{0:T(128)S(1)}) all-reduce(f32[4]{0:T(128)S(1)} %get-tuple-element.42, f32[4]{0:T(128)S(1)} %get-tuple-element.40), channel_id=1, replica_groups=mesh['shard'=8,'tensor'=4] {'shard','tensor'}, use_global_device_ids=true, to_apply=%region_4.0 | all-reduce | flops 8 | bytes 64 | tf_op jit(solution)/shard_map/psum | solution.py:61
  198.1 0.8 copy.36
  (32 shorter events, 3.9 us)
Async XLA Ops:
  7.2 84.1 %copy-start = (bf16[1,192,768]{2,1,0:T(8,128)(2,1)S(1)}, bf16[1,192,768]{2,1,0:T(8,128)(2,1)}, u32[]{:S(2)}) copy-start(bf16[1,192,768]{2,1,0:T(8,128)(2,1)} %param.14) | copy-start | bytes 884740
  7.2 32.2 %reduce-scatter.4.cloned.1.call-start = ((), (), s32[]{:S(2)}) async-start(), calls=%async_computation.6 | async-start | bytes 1474560
  10.8 30.5 %copy-start.4 = (s32[4]{0:T(128)S(1)}, s32[4]{0:T(128)}, u32[]{:S(2)}) copy-start(s32[4]{0:T(128)} %param.16) | copy-start | bytes 52
  10.8 80.5 %all-gather.4.cloned.1.call-start = ((), (), s32[]{:S(2)}) async-start(), calls=%async_computation.4 | async-start | bytes 2949120 | tf_op jit(solution)/shard_map/all_gather | solution.py:36
  40.9 1.3 copy-start.2
  69.0 41.4 %all-gather.6.cloned.1.call-start = ((), (), s32[]{:S(2)}) async-start(), calls=%async_computation.5 | async-start | bytes 1474560 | tf_op jit(solution)/shard_map/all_gather | solution.py:45
  127.7 9.3 %copy-start.5 = (f32[1,4,96]{2,1,0:T(4,128)S(1)}, f32[1,4,96]{2,1,0:T(4,128)}, u32[]{:S(2)}) copy-start(f32[1,4,96]{2,1,0:T(4,128)} %param.17) | copy-start | bytes 4612
  127.7 15.6 %copy-start.6 = (f32[4,96]{1,0:T(4,128)S(1)}, f32[4,96]{1,0:T(4,128)}, u32[]{:S(2)}) copy-start(f32[4,96]{1,0:T(4,128)} %param.19) | copy-start | bytes 4612
  127.7 15.6 %copy-start.7 = (f32[4,96]{1,0:T(4,128)S(1)}, f32[4,96]{1,0:T(4,128)}, u32[]{:S(2)}) copy-start(f32[4,96]{1,0:T(4,128)} %param.18) | copy-start | bytes 4612
  129.2 16.8 %copy-start.1 = (f32[768,768]{0,1:T(8,128)S(1)}, f32[768,768]{0,1:T(8,128)}, u32[]{:S(2)}) copy-start(f32[768,768]{0,1:T(8,128)} %all-gather.4.cloned.1.call-done) | copy-start | bytes 7077892
  131.5 25.5 %all-to-all-start.2 = ((f32[8,96,192]{2,1,0:T(8,128)}), f32[8,96,192]{2,1,0:T(8,128)}, u32[]{:S(2)}, u32[]{:S(2)}) async-start(f32[8,96,192]{2,1,0:T(8,128)} %bitcast.43), calls=%async_computation.2 | async-start | bytes 1572864 | tf_op jit(solution)/shard_map/all_to_all | solution.py:51
  143.9 6.1 %copy-start.3 = (f32[1,192,768]{2,1,0:T(8,128)S(1)}, f32[1,192,768]{2,1,0:T(8,128)}, u32[]{:S(2)}) copy-start(f32[1,192,768]{2,1,0:T(8,128)} %param.13) | copy-start | bytes 1769476
Sparse Core Ops, SparseCore 0:
  11.0 28.4 reduce-scatter.3
  69.1 22.1 all-gather.3
  93.0 17.4 all-gather.5
where the time goes:
time: 206 us; the launch traced here: 205 us
  blocking collectives  83.8 us (41%)
  waiting for transfers between devices  69.1 us (34%)
  matrix products  16 us (8%)
  local copies, waits for them, and re-layouts  14.2 us (7%)
  between operations  13.9 us (7%)
  starting transfers between devices  5.64 us (3%)
  other arithmetic  2.89 us (1%)
    psum x1, blocking collectives, local(): lax.psum((adam_sq, shampoo_local), ('shard', 'tensor'))  38 us
    unnamed x4, waiting for transfers between devices  29.3 us
    all_to_all x1, blocking collectives, local(): lax.all_to_all(outgoing, 'shard', split_axis=0, concat_axis=1, tiled=True)  25.5 us
    all_gather x1, waiting for transfers between devices, local(): whole = lax.all_gather(arrived, 'tensor', axis=1, tiled=True)  21.6 us
    all_gather x1, waiting for transfers between devices, local(): lax.all_gather(right_root[0], 'tensor', axis=0, tiled=True)  16 us
    all_to_all x1, blocking collectives, local(): lax.all_to_all(row_block[None], 'tensor', split_axis=2, concat_axis=1, ti...  14.1 us
    psum x1, blocking collectives, local(): vec_grad = lax.psum(vec_parts[0], 'tensor')  6.25 us
    unnamed x21, local copies, waits for them, and re-layouts  5.86 us
  transfers between devices with their start and end apart: 4, of which 4 were waited for; matrix products, arithmetic and copies ran while one was open for 7% of the time, Pallas kernels for 0%

commit v1 on v0

--- a/solution.py
+++ b/solution.py
@@ -33,7 +33,15 @@
     outgoing = jnp.dot(slot_hot, grad.reshape(tiles, rows_dev * cols_dev), precision=HIGH)
     outgoing = outgoing.reshape(shards, rows_dev, cols_dev)
     arrived = lax.all_to_all(outgoing, "shard", split_axis=0, concat_axis=1, tiled=True)[0]
-    whole = lax.all_gather(arrived, "tensor", axis=1, tiled=True)
+    ways, here = (lax.axis_size("tensor"), lax.axis_index("tensor"))
+    grown, reach = (arrived, 1)
+    while reach < ways:
+        theirs = lax.ppermute(grown, "tensor", [(d, d ^ reach) for d in range(ways)])
+        mine_first = jnp.concatenate([grown, theirs], axis=1)
+        theirs_first = jnp.concatenate([theirs, grown], axis=1)
+        grown = jnp.where(here & reach == 0, mine_first, theirs_first)
+        reach = 2 * reach
+    whole = grown
     start = lax.axis_index("tensor") * cols_dev
     tile_rows = lax.dynamic_slice_in_dim(whole, start, cols_dev, 0)
     new_left = STAT_DECAY * left_stat[0] + (1.0 - STAT_DECAY) * jnp.dot(

time: 206 us -> 213 us (1.034)
  local copies, waits for them, and re-layouts: 14.2 us -> 19.6 us
  other arithmetic: 2.89 us -> 5.68 us
  waiting for transfers between devices: 69.1 us -> 66.4 us
    ppermute x0 -> x2, waiting for transfers between devices: none -> 35.4 us  [local(): lax.ppermute(grown, 'tensor', [(d, d ^ reach) for d in range(ways)])]
    all_gather x1 -> x0, waiting for transfers between devices: 21.6 us -> none  [local(): whole = lax.all_gather(arrived, 'tensor', axis=1, tiled=True)]
    all_gather x1, waiting for transfers between devices: 16 us -> 0.01 us  [local(): lax.all_gather(right_root[0], 'tensor', axis=0, tiled=True)]
    all_to_all x3, local copies, waits for them, and re-layouts: 4.23 us -> 7.64 us  [local(): lax.all_to_all(row_block[None], 'tensor', split_axis=2, concat_axis=1, ti...]
    select_n x0 -> x2, other arithmetic: none -> 2.79 us  [local(): grown = jnp.where(here & reach == 0, mine_first, theirs_first)]
    broadcast_in_dim x1, local copies, waits for them, and re-layouts: 0.58 us -> 2.99 us  [local(): row_block[None]]
    unnamed x4 -> x3, waiting for transfers between devices: 29.3 us -> 28.6 us
  transfers between devices with their start and end apart: 4 -> 5, of which waited for: 4 -> 4; matrix products, arithmetic and copies ran while one was open for 7% -> 8% of each run, Pallas kernels for 0% -> 0%
where the time goes in v1:
time: 213 us
  blocking collectives  85.6 us (40%)
  waiting for transfers between devices  66.4 us (31%)
  local copies, waits for them, and re-layouts  19.6 us (9%)
  matrix products  16.1 us (8%)
  between operations  14.2 us (7%)
  other arithmetic  5.68 us (3%)
  starting transfers between devices  4.98 us (2%)
    psum x1, blocking collectives, local(): lax.psum((adam_sq, shampoo_local), ('shard', 'tensor'))  38 us
    ppermute x2, waiting for transfers between devices, local(): lax.ppermute(grown, 'tensor', [(d, d ^ reach) for d in range(ways)])  35.4 us
    unnamed x3, waiting for transfers between devices  28.6 us
    all_to_all x1, blocking collectives, local(): lax.all_to_all(outgoing, 'shard', split_axis=0, concat_axis=1, tiled=True)  25.5 us
    all_to_all x1, blocking collectives, local(): lax.all_to_all(row_block[None], 'tensor', split_axis=2, concat_axis=1, ti...  15.9 us
    all_to_all x3, local copies, waits for them, and re-layouts, local(): lax.all_to_all(row_block[None], 'tensor', split_axis=2, concat_axis=1, ti...  7.64 us
    unnamed x21, local copies, waits for them, and re-layouts  6.25 us
    psum x1, blocking collectives, local(): vec_grad = lax.psum(vec_parts[0], 'tensor')  6.25 us
  transfers between devices with their start and end apart: 5, of which 4 were waited for; matrix products, arithmetic and copies ran while one was open for 8% of the time, Pallas kernels for 0%

profile of v1, /device:TPU:0, one launch (start us, length us, event | category | flops | bytes accessed | tf_op | source)
XLA Modules:
  0.0 212.6 jit_solution(12833048876046035035)
XLA Ops:
  7.2 1.8 copy.38
  9.0 1.8 reshape.39
  10.9 28.5 %reduce-scatter.4.cloned.1.call-done = f32[192,384]{1,0:T(8,128)} async-done(((f32[768,384]{1,0:T(8,128)}), f32[192,384]{1,0:T(8,128)}) %reduce-scatter.4.cloned.1.call-update) | async-done | bytes 294928
  39.4 1.2 reshape.40
  42.4 25.5 %all_to_all.29 = f32[8,96,192]{2,1,0:T(8,128)S(1)} all-to-all(f32[8,96,192]{2,1,0:T(8,128)S(1)} %copy.30), channel_id=1, replica_groups=mesh['shard'=8,'tensor'=4] {'shard'}, dimensions={0} | all-to-all | bytes 1179648 | tf_op jit(solution)/shard_map/all_to_all | solution.py:35
  68.3 2.0 collective-permute-done
  71.4 33.5 %collective-permute-done.1 = f32[768,384]{0,1:T(8,128)} collective-permute-done((f32[768,384]{0,1:T(8,128)S(1)}, f32[768,384]{0,1:T(8,128)}, u32[]{:S(2)}, u32[]{:S(2)}) %collective-permute-start.1) | collective-permute-done | bytes 1179680 | tf_op jit(solution)/shard_map/ppermute | solution.py:39
  104.8 2.7 %maximum_select_fusion = f32[768,768]{0,1:T(8,128)S(1)} fusion(f32[768,384]{0,1:T(8,128)} %collective-permute-done.1, f32[768,384]{0,1:T(8,128)} %copy-done.1, pred[]{:T(512)S(6)} %eq.22), kind=kLoop, calls=%fused_computation | loop fusion | flops 1769472 | bytes 4718593 | tf_op jit(solution)/shard_map/jit(_where)/select_n | solution.py:42
  107.5 2.3 %fusion.11 = f32[768,192]{0,1:T(8,128)} fusion(f32[768,768]{0,1:T(8,128)S(1)} %maximum_select_fusion, bf16[1,192,768]{2,1,0:T(8,128)(2,1)S(1)} %copy-done), kind=kOutput, calls=%fused_computation.19 | convolution fusion | flops 1358954496 | bytes 3244032 | tf_op jit(solution)/shard_map/dot_general | solution.py:54
  109.8 3.1 %convolution_bitcast_fusion = f32[1,192,768]{2,1,0:T(8,128)} fusion(f32[768,192]{0,1:T(8,128)} %fusion.11, bf16[1,768,768]{2,1,0:T(8,128)(2,1)} %all-gather.3.cloned.1.call-done), kind=kOutput, calls=%fused_computation.7 | convolution fusion | flops 1358954496 | bytes 2359296 | tf_op jit(solution)/shard_map/dot_general | solution.py:55
  113.0 3.0 %copy.32 = f32[1,192,768]{1,0,2:T(1,128)} copy(f32[1,192,768]{2,1,0:T(8,128)} %convolution_bitcast_fusion) | data formatting | bytes 1179648 | tf_op jit(solution)/shard_map/broadcast_in_dim | solution.py:56
  115.9 15.9 %all_to_all.30 = f32[1,192,768]{1,0,2:T(1,128)} all-to-all(f32[1,192,768]{1,0,2:T(1,128)} %copy.32), channel_id=1, replica_groups=mesh['shard'=8,'tensor'=4] {'tensor'}, dimensions={2} | all-to-all | bytes 1179648 | tf_op jit(solution)/shard_map/all_to_all | solution.py:56
  131.9 2.9 %copy.33 = f32[1,192,768]{2,1,0:T(8,128)} copy(f32[1,192,768]{1,0,2:T(1,128)} %all_to_all.30) | data formatting | bytes 1179648 | tf_op jit(solution)/shard_map/all_to_all | solution.py:56
  134.8 2.6 %all_to_all.23 = f32[1,192,4,192]{3,2,1,0:T(4,128)} reshape(f32[1,192,768]{2,1,0:T(8,128)} %copy.33) | data formatting | bytes 1179648 | tf_op jit(solution)/shard_map/all_to_all | solution.py:56
  137.3 2.2 %copy.34 = f32[1,4,192,192]{3,2,1,0:T(8,128)} copy(f32[1,4,192,192]{3,1,2,0:T(4,128)} %bitcast.44) | data formatting | bytes 1179648 | tf_op jit(solution)/shard_map/all_to_all | solution.py:56
  139.5 4.2 %all-to-all-start.2 = ((f32[8,96,192]{2,1,0:T(8,128)}), f32[8,96,192]{2,1,0:T(8,128)}, u32[]{:S(2)}, u32[]{:S(2)}) async-start(f32[8,96,192]{2,1,0:T(8,128)} %bitcast.43), calls=%async_computation.2 | async-start | bytes 1572864 | tf_op jit(solution)/shard_map/all_to_all | solution.py:59
  143.7 6.2 %psum.23 = f32[4,96]{1,0:T(4,128)S(1)} all-reduce(f32[4,96]{1,0:T(4,128)S(1)} %bitcast.49), channel_id=1, replica_groups=mesh['shard'=8,'tensor'=4] {'tensor'}, use_global_device_ids=true, to_apply=%region_5.6 | all-reduce | flops 384 | bytes 3072 | tf_op jit(solution)/shard_map/psum | solution.py:27
  150.6 2.1 %multiply_reduce_fusion.1 = (f32[4]{0:T(128)S(1)}, f32[4,96,192]{2,1,0:T(8,128)}) fusion(f32[4,96,192]{2,1,0:T(8,128)} %copy-done.2, f32[4,96,192]{2,1,0:T(8,128)} %param.11), kind=kLoop, calls=%fused_computation.18 | loop fusion | flops 663548 | bytes 884752 | tf_op jit(solution)/shard_map/reduce_sum | solution.py:26
  152.7 4.0 %fusion.3 = f32[1,192,768]{2,1,0:T(8,128)} fusion(f32[768,768]{0,1:T(8,128)S(1)} %maximum_select_fusion, s32[]{:T(128)S(6)} %select_n.23, f32[1,192,768]{2,1,0:T(8,128)} %param.12), kind=kOutput, calls=%fused_computation.6 | convolution fusion | flops 1359396864 | bytes 4325380 | tf_op jit(solution)/shard_map/dot_general | solution.py:47
  156.7 4.8 %fusion.1 = f32[1,192,768]{2,1,0:T(8,128)} fusion(f32[768,192]{1,0:T(8,128)S(1)} %bitcast.41, f32[768,768]{0,1:T(8,128)S(1)} %maximum_select_fusion, f32[1,192,768]{2,1,0:T(8,128)S(1)} %copy-done.3), kind=kOutput, calls=%fused_computation.3 | convolution fusion | flops 1359396864 | bytes 4128768 | tf_op jit(solution)/shard_map/dot_general | solution.py:50
  161.5 2.4 %all-to-all-done.2 = f32[8,96,192]{2,1,0:T(8,128)} async-done(((f32[8,96,192]{2,1,0:T(8,128)}), f32[8,96,192]{2,1,0:T(8,128)}, u32[]{:S(2)}, u32[]{:S(2)}) %all-to-all-start.2) | async-done | bytes 589856 | tf_op jit(solution)/shard_map/all_to_all | solution.py:59
  163.9 1.4 reshape.36
  165.7 1.1 multiply_reduce_fusion
  166.8 38.0 %all-reduce = (f32[4]{0:T(128)S(1)}, f32[4]{0:T(128)S(1)}) all-reduce(f32[4]{0:T(128)S(1)} %get-tuple-element.42, f32[4]{0:T(128)S(1)} %get-tuple-element.40), channel_id=1, replica_groups=mesh['shard'=8,'tensor'=4] {'shard','tensor'}, use_global_device_ids=true, to_apply=%region_4.5 | all-reduce | flops 8 | bytes 64 | tf_op jit(solution)/shard_map/psum | solution.py:69
  (35 shorter events, 5.2 us)
Async XLA Ops:
  7.2 100.4 %copy-start = (bf16[1,192,768]{2,1,0:T(8,128)(2,1)S(1)}, bf16[1,192,768]{2,1,0:T(8,128)(2,1)}, u32[]{:S(2)}) copy-start(bf16[1,192,768]{2,1,0:T(8,128)(2,1)} %param.14) | copy-start | bytes 884740
  7.2 32.2 %reduce-scatter.4.cloned.1.call-start = ((), (), s32[]{:S(2)}) async-start(), calls=%async_computation.5 | async-start | bytes 1474560
  10.8 30.5 %copy-start.4 = (s32[4]{0:T(128)S(1)}, s32[4]{0:T(128)}, u32[]{:S(2)}) copy-start(s32[4]{0:T(128)} %param.16) | copy-start | bytes 52
  10.8 99.0 %all-gather.3.cloned.1.call-start = ((), (), s32[]{:S(2)}) async-start(), calls=%async_computation.4 | async-start | bytes 1474560 | tf_op jit(solution)/shard_map/all_gather | solution.py:53
  40.8 1.3 copy-start.2
  68.2 2.1 collective-permute-start
  70.3 1.0 copy-start.1
  70.3 34.5 %collective-permute-start.1 = (f32[768,384]{0,1:T(8,128)S(1)}, f32[768,384]{0,1:T(8,128)}, u32[]{:S(2)}, u32[]{:S(2)}) collective-permute-start(f32[768,384]{0,1:T(8,128)S(1)} %maximum_select_fusion.1), channel_id=1, source_target_pairs={{0,2},{1,3},{2,0},{3,1},{4,6},{5,7},{6,4},{7,5},{8,10},{9,11},{10,... | collective-permute-start | bytes 3538952 | tf_op jit(solution)/shard_map/ppermute | solution.py:39
  134.8 9.0 %copy-start.5 = (f32[1,4,96]{2,1,0:T(4,128)S(1)}, f32[1,4,96]{2,1,0:T(4,128)}, u32[]{:S(2)}) copy-start(f32[1,4,96]{2,1,0:T(4,128)} %param.17) | copy-start | bytes 4612
  134.8 15.2 %copy-start.6 = (f32[4,96]{1,0:T(4,128)S(1)}, f32[4,96]{1,0:T(4,128)}, u32[]{:S(2)}) copy-start(f32[4,96]{1,0:T(4,128)} %param.19) | copy-start | bytes 4612
  134.8 15.2 %copy-start.7 = (f32[4,96]{1,0:T(4,128)S(1)}, f32[4,96]{1,0:T(4,128)}, u32[]{:S(2)}) copy-start(f32[4,96]{1,0:T(4,128)} %param.18) | copy-start | bytes 4612
  139.5 24.4 %all-to-all-start.2 = ((f32[8,96,192]{2,1,0:T(8,128)}), f32[8,96,192]{2,1,0:T(8,128)}, u32[]{:S(2)}, u32[]{:S(2)}) async-start(f32[8,96,192]{2,1,0:T(8,128)} %bitcast.43), calls=%async_computation.2 | async-start | bytes 1572864 | tf_op jit(solution)/shard_map/all_to_all | solution.py:59
  150.6 6.1 %copy-start.3 = (f32[1,192,768]{2,1,0:T(8,128)S(1)}, f32[1,192,768]{2,1,0:T(8,128)}, u32[]{:S(2)}) copy-start(f32[1,192,768]{2,1,0:T(8,128)} %param.13) | copy-start | bytes 1769476
Sparse Core Ops, SparseCore 0:
  10.9 28.4 reduce-scatter.3
  68.4 22.1 all-gather.2
